TPU v7x, 32 devices: a whole 2x2x4 slice. The times are simulated.
32 devices in a mesh: groups: 2 (over x), gx: 4 (over y, core), gy: 4 (over z).
Axes of the slice: x: 2, y: 2, z: 4, core: 2. Of those that a mesh axis runs over, the one named last changes fastest.
Arguments:
- features: bfloat16 [8, 4, 4, 64, 256], P(('groups', 'gx'), 'gy'), parts along dimension 0, may hold values from -6 to 6
- neighbour_table: int32 [8, 4, 4, 27], P(('groups', 'gx'), 'gy'), parts along dimension 0, may hold values from 0 to 36, as said below
- kernel_weight: bfloat16 [27, 256, 256], replicated, may hold values from -0.078125 to 0.078125
- out_cotangent: bfloat16 [8, 4, 4, 64, 256], P(('groups', 'gx'), 'gy'), parts along dimension 0, may hold values from -6 to 6
Outputs:
- out_features: bfloat16 [8, 4, 4, 64, 256], P(('groups', 'gx'), 'gy'), parts along dimension 0
- grad_features: bfloat16 [8, 4, 4, 64, 256], P(('groups', 'gx'), 'gy'), parts along dimension 0
- grad_kernel: float32 [13824, 256], P(('groups', 'gx')), parts along dimension 0
There are 2 independent parts, one for each index of `groups`. A program takes and returns all parts, laid end to end along the dimension named above; an argument that names none is the same for every part. Nothing has to cross between parts.
Inputs may be any that keep to these rules, and one draw needn't show every extreme that they name: `neighbour_table`: within a tile the live slots come first; an empty slot has all 27 entries equal to 36; a live slot s has entry 16 + s at offset 13; adjacency is symmetric; some tile has all 4 slots live and the live counts differ much between tiles.
All inputs are finite; a program needn't handle non-finite values.
Results may differ from a plain program's by a relative error of at most 0.001.
Values may be sent and summed in bfloat16 or wider, within the bound.
A program may use at most 128 MiB of HBM per device.

v0:
```python
import jax
import jax.numpy as jnp
from jax import lax
from jax.sharding import PartitionSpec as P

kernel_scale = 0.00390625
offset_list = [
    (first_step, second_step, third_step)
    for first_step in (-1, 0, 1)
    for second_step in (-1, 0, 1)
    for third_step in (-1, 0, 1)
]
source_spans = ((3, 4), (0, 4), (0, 1))


def extended_2(array, sides, width):
    for axis, dim in sides:
        size, length = (lax.axis_size(axis), array.shape[dim])
        up = [(i, (i + 1) % size) for i in range(size - 1)]
        down = [(j, i) for i, j in up]
        last = lax.slice_in_dim(array, length - width, length, axis=dim)
        initial = lax.slice_in_dim(array, 0, width, axis=dim)
        before = lax.ppermute(last, axis, up)
        after = lax.ppermute(initial, axis, down)
        array = jnp.concatenate([before, array, after], axis=dim)
    return array


def assemble_block(extended, brick_table):
    slot_total = brick_table.shape[0]
    channels = extended.shape[-1]
    bricks = extended.reshape(extended.shape[0], 4, 4, 4, channels)
    fetched = jnp.take(bricks, brick_table.reshape(-1), axis=0).reshape(
        slot_total, 27, 4, 4, 4, channels
    )
    planes = []
    for first_step in (-1, 0, 1):
        rows_list = []
        for second_step in (-1, 0, 1):
            pieces = []
            for third_step in (-1, 0, 1):
                offset_index = ((first_step + 1) * 3 + (second_step + 1)) * 3 + (third_step + 1)
                source_x = source_spans[first_step + 1]
                source_y = source_spans[second_step + 1]
                source_z = source_spans[third_step + 1]
                pieces.append(
                    fetched[
                        :,
                        offset_index,
                        source_x[0] : source_x[1],
                        source_y[0] : source_y[1],
                        source_z[0] : source_z[1],
                        :,
                    ]
                )
            rows_list.append(jnp.concatenate(pieces, axis=3))
        planes.append(jnp.concatenate(rows_list, axis=2))
    return jnp.concatenate(planes, axis=1)


def window(padded, shift, sign):
    channels = padded.shape[-1]
    lower = [1 + sign * value for value in shift]
    return padded[
        :, lower[0] : lower[0] + 4, lower[1] : lower[1] + 4, lower[2] : lower[2] + 4, :
    ].reshape(-1, channels)


def forward_conv(padded, kernel_weight):
    summed = None
    for offset_index, shift in enumerate(offset_list):
        product = jnp.dot(
            window(padded, shift, 1),
            kernel_weight[offset_index],
            preferred_element_type=jnp.float32,
        )
        summed = product if summed is None else summed + product
    return summed


def pull_conv(cot_padded, kernel_weight):
    summed = None
    for offset_index, shift in enumerate(offset_list):
        product = lax.dot_general(
            window(cot_padded, shift, -1),
            kernel_weight[offset_index],
            (((1,), (1,)), ((), ())),
            preferred_element_type=jnp.float32,
        )
        summed = product if summed is None else summed + product
    return summed


def kernel_term(padded, cot_flat):
    blocks_list = []
    for offset_index, shift in enumerate(offset_list):
        blocks_list.append(
            lax.dot_general(
                window(padded, shift, 1),
                cot_flat,
                (((0,), (0,)), ((), ())),
                preferred_element_type=jnp.float32,
            )
        )
    return jnp.concatenate(blocks_list, axis=0) * kernel_scale


def widen(beside_all, slot_count, voxels, channels):
    flat = beside_all.reshape(9 * slot_count, voxels, channels)
    return jnp.concatenate([flat, jnp.zeros((1, voxels, channels), beside_all.dtype)], axis=0)


def body(features, neighbour_table, kernel_weight, out_cotangent):
    slot_count = features.shape[2]
    voxels = features.shape[3]
    channels = features.shape[4]
    brick_table = neighbour_table[0, 0]
    beside_all = extended_2(features, (("gx", 0), ("gy", 1)), 1)
    padded = assemble_block(widen(beside_all, slot_count, voxels, channels), brick_table)
    out_flat = forward_conv(padded, kernel_weight).astype(jnp.bfloat16)
    cot_flat = out_cotangent.reshape(slot_count * voxels, channels)
    kernel_part = kernel_term(padded, cot_flat)
    row_part = lax.psum_scatter(kernel_part, "gx", scatter_dimension=0, tiled=True)
    grad_kernel = lax.psum(row_part, "gy")
    cot_around = extended_2(out_cotangent, (("gx", 0), ("gy", 1)), 1)
    cot_padded = assemble_block(widen(cot_around, slot_count, voxels, channels), brick_table)
    grad_flat = pull_conv(cot_padded, kernel_weight).astype(jnp.bfloat16)
    return (out_flat.reshape(features.shape), grad_flat.reshape(features.shape), grad_kernel)


def solution(mesh):
    in_specs = (
        P(("groups", "gx"), "gy", None, None, None),
        P(("groups", "gx"), "gy", None, None),
        P(),
        P(("groups", "gx"), "gy", None, None, None),
    )
    out_specs = (
        P(("groups", "gx"), "gy", None, None, None),
        P(("groups", "gx"), "gy", None, None, None),
        P(("groups", "gx"), None),
    )
    return jax.shard_map(body, mesh=mesh, in_specs=in_specs, out_specs=out_specs, check_vma=False)
```

profile of v0, /device:TPU:0, one launch (start us, length us, event | category | flops | bytes accessed | tf_op | source)
XLA Modules:
  0.0 246.7 jit_solution(3739958742048851636)
XLA Ops:
  7.2 2.4 collective-permute-start
  9.6 1.3 collective-permute-start.1
  10.9 1.3 collective-permute-start.5
  12.2 5.8 %collective-permute-start.4 = (bf16[1,1,4,64,256]{4,3,2,1,0:T(8,128)(2,1)}, bf16[1,1,4,64,256]{4,3,2,1,0:T(8,128)(2,1)S(1)}, u32[]{:S(2)}, u32[]{:S(2)}) collective-permute-start(bf16[1,1,4,64,256]{4,3,2,1,0:T(8,128)(2,1)} %param.9), channel_id=1, source_target_pairs={{0,4},{4,8},{8,12},{1,5},{5,9},{9,13},{2,6},{6,10},{10,14},{3,7},{... | collective-permute-start | bytes 393224 | tf_op jit(solution)/shard_map/ppermute | solution.py:23
  18.8 0.9 constant_dynamic-update-slice_fusion.1
  19.7 1.3 collective-permute-start.3
  21.0 4.6 %collective-permute-start.2 = (bf16[3,1,4,64,256]{4,3,2,1,0:T(8,128)(2,1)S(1)}, bf16[3,1,4,64,256]{4,3,2,1,0:T(8,128)(2,1)S(1)}, u32[]{:S(2)}, u32[]{:S(2)}) collective-permute-start(bf16[3,1,4,64,256]{4,3,2,1,0:T(8,128)(2,1)S(1)} %constant_dynamic-update-slice_fusion), channel_id=1, source_target_pairs={{0,1},{1,2},{2,3},{4,5},{5,6},{6,7},{8,9},{9,10},{10,11},{12,13},{... | collective-permute-start | bytes 1179656 | tf_op jit(solution)/shard_map/ppermute | solution.py:23
  26.6 1.3 collective-permute-start.7
  27.9 5.3 %collective-permute-start.6 = (bf16[3,1,4,64,256]{4,3,2,1,0:T(8,128)(2,1)S(1)}, bf16[3,1,4,64,256]{4,3,2,1,0:T(8,128)(2,1)}, u32[]{:S(2)}, u32[]{:S(2)}) collective-permute-start(bf16[3,1,4,64,256]{4,3,2,1,0:T(8,128)(2,1)S(1)} %constant_dynamic-update-slice_fusion.3), channel_id=1, source_target_pairs={{0,1},{1,2},{2,3},{4,5},{5,6},{6,7},{8,9},{9,10},{10,11},{12,13},{... | collective-permute-start | bytes 1179656 | tf_op jit(solution)/shard_map/ppermute | solution.py:23
  33.2 1.5 collective-permute-done.2
  35.2 6.1 %collective-permute-done.7 = bf16[3,1,4,64,256]{4,3,2,1,0:T(8,128)(2,1)S(1)} collective-permute-done((bf16[3,1,4,64,256]{4,3,2,1,0:T(8,128)(2,1)S(1)}, bf16[3,1,4,64,256]{4,3,2,1,0:T(8,128)(2,1)S(1)}, u32[]{:S(2)}, u32[]{:S(2)}) %collective-permute-start.7) | collective-permute-done | bytes 393248 | tf_op jit(solution)/shard_map/ppermute | solution.py:24
  41.3 1.8 collective-permute-done.6
  43.1 1.1 pad_maximum_fusion.1
  44.2 1.2 concatenate.194
  45.4 2.5 %reshape.251 = bf16[37,4,4,4,256]{4,3,2,1,0:T(4,128)(2,1)S(1)} reshape(bf16[37,64,256]{2,1,0:T(8,128)(2,1)} %concatenate.194) | data formatting | bytes 2424832 | tf_op jit(solution)/shard_map/reshape | solution.py:32
  47.9 7.1 %gather_fusion.1 = bf16[108,4,4,4,256]{4,3,2,1,0:T(4,128)(2,1)} fusion(bf16[37,4,4,4,256]{4,3,2,1,0:T(4,128)(2,1)S(1)} %reshape.251, s32[1024]{0:T(1024)S(1)} %pad_clamp_fusion), kind=kCustom, calls=%fused_computation.1.clone | custom fusion | bytes 7078320 | tf_op jit(solution)/shard_map/jit(_take)/gather | solution.py:33
  55.0 7.2 %gather_fusion = bf16[108,4,4,4,256]{4,3,2,1,0:T(4,128)(2,1)} fusion(bf16[37,4,4,4,256]{4,3,2,1,0:T(4,128)(2,1)S(1)} %reshape.221, s32[1024]{0:T(1024)S(1)} %pad_clamp_fusion), kind=kCustom, calls=%fused_computation.clone | custom fusion | bytes 7078320 | tf_op jit(solution)/shard_map/jit(_take)/gather | solution.py:33
  62.3 6.4 %broadcast_select_fusion = (bf16[108,4,4,4,256]{4,3,2,1,0:T(4,128)(2,1)S(1)}, bf16[108,4,4,4,256]{4,3,2,1,0:T(4,128)(2,1)S(1)}) fusion(bf16[108,4,4,4,256]{4,3,2,1,0:T(4,128)(2,1)} %gather_fusion.1, pred[108]{0:T(512)(128)(4,1)S(1)} %compare_and_fusion, bf16[108,4,4,4,256]{4,3,2,1,0:T(4,128)(2,1)} %gather_fusion), kind=kLoop, calls=%fused_computation.3 | loop fusion | flops 3538944 | bytes 14155884 | tf_op jit(solution)/shard_map/jit(_take)/select_n | solution.py:33
  69.2 1.2 slice_bitcast_fusion.1
  76.8 1.3 fusion.116
  78.1 1.0 reshape.247
  79.1 1.0 reshape.246
  80.3 1.0 reshape.240
  81.3 1.2 convolution_dynamic-update-slice_fusion.26
  82.5 1.1 convolution_dynamic-update-slice_fusion.25
  83.7 1.1 convolution_dynamic-update-slice_fusion.24
  90.4 3.3 %broadcast_multiply_fusion = f32[6912,256]{1,0:T(8,128)} fusion(f32[6912,256]{1,0:T(8,128)S(1)} %convolution_dynamic-update-slice_fusion), kind=kLoop, calls=%fused_computation.2 | loop fusion | flops 1769472 | bytes 14155776 | tf_op jit(solution)/shard_map/mul | solution.py:105
  107.4 1.3 maximum_maximum_fusion.1
  108.7 1.4 fusion.114
  110.2 1.8 reshape.271
  112.0 1.6 reshape.270
  113.5 3.9 %fusion.115 = (bf16[4,4,4,4,256]{4,3,2,1,0:T(4,128)(2,1)}, bf16[4,4,4,4,256]{4,3,2,1,0:T(4,128)(2,1)}, bf16[4,4,4,4,256]{4,3,2,1,0:T(4,128)(2,1)}, bf16[4,4,4,4,...) fusion(bf16[4,5,6,6,256]{4,3,2,1,0:T(8,128)(2,1)} %get-tuple-el, ...), kind=kLoop, calls=%fused_computation.284 | loop fusion | bytes 2359296 | tf_op jit(solution)/shard_map/slice | solution.py:64
  117.4 1.6 reshape.261
  119.1 1.6 reshape.260
  120.7 1.6 reshape.259
  122.2 1.6 reshape.258
  123.8 1.6 reshape.257
  125.4 1.6 reshape.256
  127.0 1.6 reshape.255
  128.6 1.6 reshape.254
  130.2 1.6 reshape.253
  131.8 1.1 fusion.56
  133.0 1.2 fusion.54
  134.1 1.1 convolution_add_fusion.51
  135.3 1.1 convolution_add_fusion.50
  136.4 1.1 convolution_add_fusion.49
  137.6 1.1 convolution_add_fusion.48
  148.3 0.9 convolution_add_fusion.7
  149.3 9.7 %reduce-scatter.2.cloned.1.call-done = f32[1728,256]{1,0:T(8,128)} async-done(((f32[6912,256]{1,0:T(8,128)}), f32[1728,256]{1,0:T(8,128)}) %reduce-scatter.2.cloned.1.call-update) | async-done | bytes 1769488 | tf_op jit(solution)/shard_map/reduce_scatter | solution.py:123
  159.0 1.9 fusion
  160.9 1.6 reshape.278
  162.5 1.6 reshape.277
  164.1 1.6 reshape.276
  165.6 1.6 reshape.275
  167.2 1.6 reshape.274
  168.8 1.6 reshape.273
  170.4 1.6 reshape.272
  172.0 1.3 convolution_add_fusion.6
  173.3 1.1 convolution_add_fusion.5
  174.4 1.1 convolution_add_fusion.4
  175.6 1.1 convolution_add_fusion.3
  176.7 1.1 convolution_add_fusion.2
  179.0 58.1 %all-reduce.4.cloned.1.call-done = f32[1728,256]{1,0:T(8,128)} async-done(((f32[1728,256]{1,0:T(8,128)}), f32[1728,256]{1,0:T(8,128)}) %all-reduce.4.cloned.1.call-update) | async-done | bytes 1769488 | tf_op jit(solution)/shard_map/psum | solution.py:124
  237.1 2.8 %copy.210 = f32[1728,256]{1,0:T(8,128)} copy(f32[1728,256]{1,0:T(8,128)} %all-reduce.4.cloned.1.call-done) | data formatting | bytes 3538944
  (294 shorter events, 37.8 us)
Async XLA Ops:
  7.2 151.8 %reduce-scatter.2.cloned.1.call-start = ((), (), s32[]{:S(2)}) async-start(), calls=%async_computation.1 | async-start | bytes 8847360 | tf_op jit(solution)/shard_map/reduce_scatter | solution.py:123
  7.2 11.6 %collective-permute-start = (bf16[1,1,4,64,256]{4,3,2,1,0:T(8,128)(2,1)}, bf16[1,1,4,64,256]{4,3,2,1,0:T(8,128)(2,1)S(1)}, u32[]{:S(2)}, u32[]{:S(2)}) collective-permute-start(bf16[1,1,4,64,256]{4,3,2,1,0:T(8,128)(2,1)} %param.6), channel_id=1, source_target_pairs={{0,4},{4,8},{8,12},{1,5},{5,9},{9,13},{2,6},{6,10},{10,14},{3,7},{... | collective-permute-start | bytes 393224 | tf_op jit(solution)/shard_map/ppermute | solution.py:23
  9.6 10.1 %collective-permute-start.1 = (bf16[1,1,4,64,256]{4,3,2,1,0:T(8,128)(2,1)}, bf16[1,1,4,64,256]{4,3,2,1,0:T(8,128)(2,1)S(1)}, u32[]{:S(2)}, u32[]{:S(2)}) collective-permute-start(bf16[1,1,4,64,256]{4,3,2,1,0:T(8,128)(2,1)} %param.6), channel_id=1, source_target_pairs={{4,0},{8,4},{12,8},{5,1},{9,5},{13,9},{6,2},{10,6},{14,10},{7,3},{... | collective-permute-start | bytes 393224 | tf_op jit(solution)/shard_map/ppermute | solution.py:24
  10.9 15.7 %collective-permute-start.5 = (bf16[1,1,4,64,256]{4,3,2,1,0:T(8,128)(2,1)}, bf16[1,1,4,64,256]{4,3,2,1,0:T(8,128)(2,1)S(1)}, u32[]{:S(2)}, u32[]{:S(2)}) collective-permute-start(bf16[1,1,4,64,256]{4,3,2,1,0:T(8,128)(2,1)} %param.9), channel_id=1, source_target_pairs={{4,0},{8,4},{12,8},{5,1},{9,5},{13,9},{6,2},{10,6},{14,10},{7,3},{... | collective-permute-start | bytes 393224 | tf_op jit(solution)/shard_map/ppermute | solution.py:24
  12.2 13.4 %collective-permute-start.4 = (bf16[1,1,4,64,256]{4,3,2,1,0:T(8,128)(2,1)}, bf16[1,1,4,64,256]{4,3,2,1,0:T(8,128)(2,1)S(1)}, u32[]{:S(2)}, u32[]{:S(2)}) collective-permute-start(bf16[1,1,4,64,256]{4,3,2,1,0:T(8,128)(2,1)} %param.9), channel_id=1, source_target_pairs={{0,4},{4,8},{8,12},{1,5},{5,9},{9,13},{2,6},{6,10},{10,14},{3,7},{... | collective-permute-start | bytes 393224 | tf_op jit(solution)/shard_map/ppermute | solution.py:23
  19.7 13.5 %collective-permute-start.3 = (bf16[3,1,4,64,256]{4,3,2,1,0:T(8,128)(2,1)S(1)}, bf16[3,1,4,64,256]{4,3,2,1,0:T(8,128)(2,1)S(1)}, u32[]{:S(2)}, u32[]{:S(2)}) collective-permute-start(bf16[3,1,4,64,256]{4,3,2,1,0:T(8,128)(2,1)S(1)} %constant_dynamic-update-slice_fusion), channel_id=1, source_target_pairs={{1,0},{2,1},{3,2},{5,4},{6,5},{7,6},{9,8},{10,9},{11,10},{13,12},{... | collective-permute-start | bytes 1179656 | tf_op jit(solution)/shard_map/ppermute | solution.py:24
  21.0 13.6 %collective-permute-start.2 = (bf16[3,1,4,64,256]{4,3,2,1,0:T(8,128)(2,1)S(1)}, bf16[3,1,4,64,256]{4,3,2,1,0:T(8,128)(2,1)S(1)}, u32[]{:S(2)}, u32[]{:S(2)}) collective-permute-start(bf16[3,1,4,64,256]{4,3,2,1,0:T(8,128)(2,1)S(1)} %constant_dynamic-update-slice_fusion), channel_id=1, source_target_pairs={{0,1},{1,2},{2,3},{4,5},{5,6},{6,7},{8,9},{9,10},{10,11},{12,13},{... | collective-permute-start | bytes 1179656 | tf_op jit(solution)/shard_map/ppermute | solution.py:23
  26.6 14.7 %collective-permute-start.7 = (bf16[3,1,4,64,256]{4,3,2,1,0:T(8,128)(2,1)S(1)}, bf16[3,1,4,64,256]{4,3,2,1,0:T(8,128)(2,1)S(1)}, u32[]{:S(2)}, u32[]{:S(2)}) collective-permute-start(bf16[3,1,4,64,256]{4,3,2,1,0:T(8,128)(2,1)S(1)} %constant_dynamic-update-slice_fusion.3), channel_id=1, source_target_pairs={{1,0},{2,1},{3,2},{5,4},{6,5},{7,6},{9,8},{10,9},{11,10},{13,12},{... | collective-permute-start | bytes 1179656 | tf_op jit(solution)/shard_map/ppermute | solution.py:24
  27.9 15.2 %collective-permute-start.6 = (bf16[3,1,4,64,256]{4,3,2,1,0:T(8,128)(2,1)S(1)}, bf16[3,1,4,64,256]{4,3,2,1,0:T(8,128)(2,1)}, u32[]{:S(2)}, u32[]{:S(2)}) collective-permute-start(bf16[3,1,4,64,256]{4,3,2,1,0:T(8,128)(2,1)S(1)} %constant_dynamic-update-slice_fusion.3), channel_id=1, source_target_pairs={{0,1},{1,2},{2,3},{4,5},{5,6},{6,7},{8,9},{9,10},{10,11},{12,13},{... | collective-permute-start | bytes 1179656 | tf_op jit(solution)/shard_map/ppermute | solution.py:23
  71.3 15.8 %copy-start.4 = (bf16[256,256]{1,0:T(8,128)(2,1)}, bf16[256,256]{1,0:T(8,128)(2,1)S(1)}, u32[]{:S(2)}) copy-start(bf16[256,256]{1,0:T(8,128)(2,1)S(1)} %reshape_squeeze.12) | copy-start | bytes 393220
  71.6 15.7 %copy-start.6 = (bf16[256,256]{1,0:T(8,128)(2,1)}, bf16[256,256]{1,0:T(8,128)(2,1)S(1)}, u32[]{:S(2)}) copy-start(bf16[256,256]{1,0:T(8,128)(2,1)S(1)} %reshape.236) | copy-start | bytes 393220
  71.7 15.2 %copy-start.8 = (bf16[256,256]{1,0:T(8,128)(2,1)}, bf16[256,256]{1,0:T(8,128)(2,1)S(1)}, u32[]{:S(2)}) copy-start(bf16[256,256]{1,0:T(8,128)(2,1)S(1)} %reshape.235) | copy-start | bytes 393220
  73.1 15.0 %copy-start.10 = (bf16[256,256]{1,0:T(8,128)(2,1)}, bf16[256,256]{1,0:T(8,128)(2,1)S(1)}, u32[]{:S(2)}) copy-start(bf16[256,256]{1,0:T(8,128)(2,1)S(1)} %reshape.239) | copy-start | bytes 393220
  73.1 14.7 %copy-start.12 = (bf16[256,256]{1,0:T(8,128)(2,1)}, bf16[256,256]{1,0:T(8,128)(2,1)S(1)}, u32[]{:S(2)}) copy-start(bf16[256,256]{1,0:T(8,128)(2,1)S(1)} %reshape.238) | copy-start | bytes 393220
  73.2 14.4 %copy-start.14 = (bf16[256,256]{1,0:T(8,128)(2,1)}, bf16[256,256]{1,0:T(8,128)(2,1)S(1)}, u32[]{:S(2)}) copy-start(bf16[256,256]{1,0:T(8,128)(2,1)S(1)} %reshape.237) | copy-start | bytes 393220
  73.2 13.0 %copy-start.20 = (bf16[256,256]{1,0:T(8,128)(2,1)}, bf16[256,256]{1,0:T(8,128)(2,1)S(1)}, u32[]{:S(2)}) copy-start(bf16[256,256]{1,0:T(8,128)(2,1)S(1)} %reshape.232) | copy-start | bytes 393220
  73.3 13.1 %copy-start.16 = (bf16[256,256]{1,0:T(8,128)(2,1)}, bf16[256,256]{1,0:T(8,128)(2,1)S(1)}, u32[]{:S(2)}) copy-start(bf16[256,256]{1,0:T(8,128)(2,1)S(1)} %reshape.233) | copy-start | bytes 393220
  73.3 13.3 %copy-start.18 = (bf16[256,256]{1,0:T(8,128)(2,1)}, bf16[256,256]{1,0:T(8,128)(2,1)S(1)}, u32[]{:S(2)}) copy-start(bf16[256,256]{1,0:T(8,128)(2,1)S(1)} %reshape.234) | copy-start | bytes 393220
  74.4 7.0 %copy-start = (bf16[1,1,4,64,256]{4,3,2,1,0:T(8,128)(2,1)S(1)}, bf16[1,1,4,64,256]{4,3,2,1,0:T(8,128)(2,1)}, u32[]{:S(2)}) copy-start(bf16[1,1,4,64,256]{4,3,2,1,0:T(8,128)(2,1)} %param.9) | copy-start | bytes 393220
  74.4 11.6 %copy-start.30 = (bf16[256,256]{1,0:T(8,128)(2,1)}, bf16[256,256]{1,0:T(8,128)(2,1)S(1)}, u32[]{:S(2)}) copy-start(bf16[256,256]{1,0:T(8,128)(2,1)S(1)} %reshape.231) | copy-start | bytes 393220
  74.5 11.3 %copy-start.34 = (bf16[256,256]{1,0:T(8,128)(2,1)}, bf16[256,256]{1,0:T(8,128)(2,1)S(1)}, u32[]{:S(2)}) copy-start(bf16[256,256]{1,0:T(8,128)(2,1)S(1)} %reshape.230) | copy-start | bytes 393220
  74.5 11.0 %copy-start.38 = (bf16[256,256]{1,0:T(8,128)(2,1)}, bf16[256,256]{1,0:T(8,128)(2,1)S(1)}, u32[]{:S(2)}) copy-start(bf16[256,256]{1,0:T(8,128)(2,1)S(1)} %reshape.229) | copy-start | bytes 393220
  74.5 10.7 %copy-start.42 = (bf16[256,256]{1,0:T(8,128)(2,1)}, bf16[256,256]{1,0:T(8,128)(2,1)S(1)}, u32[]{:S(2)}) copy-start(bf16[256,256]{1,0:T(8,128)(2,1)S(1)} %reshape.228) | copy-start | bytes 393220
  74.6 10.4 %copy-start.46 = (bf16[256,256]{1,0:T(8,128)(2,1)}, bf16[256,256]{1,0:T(8,128)(2,1)S(1)}, u32[]{:S(2)}) copy-start(bf16[256,256]{1,0:T(8,128)(2,1)S(1)} %reshape.227) | copy-start | bytes 393220
  74.6 10.1 %copy-start.47 = (bf16[256,256]{1,0:T(8,128)(2,1)}, bf16[256,256]{1,0:T(8,128)(2,1)S(1)}, u32[]{:S(2)}) copy-start(bf16[256,256]{1,0:T(8,128)(2,1)S(1)} %reshape.226) | copy-start | bytes 393220
  78.1 12.1 %copy-start.3 = (bf16[256,256]{1,0:T(8,128)(2,1)}, bf16[256,256]{1,0:T(8,128)(2,1)S(1)}, u32[]{:S(2)}) copy-start(bf16[256,256]{1,0:T(8,128)(2,1)S(1)} %reshape.248) | copy-start | bytes 393220
  79.1 10.9 %copy-start.22 = (bf16[256,256]{1,0:T(8,128)(2,1)}, bf16[256,256]{1,0:T(8,128)(2,1)S(1)}, u32[]{:S(2)}) copy-start(bf16[256,256]{1,0:T(8,128)(2,1)S(1)} %reshape.247) | copy-start | bytes 393220
  80.1 9.7 %copy-start.24 = (bf16[256,256]{1,0:T(8,128)(2,1)}, bf16[256,256]{1,0:T(8,128)(2,1)S(1)}, u32[]{:S(2)}) copy-start(bf16[256,256]{1,0:T(8,128)(2,1)S(1)} %reshape.246) | copy-start | bytes 393220
  80.1 9.4 %copy-start.26 = (bf16[256,256]{1,0:T(8,128)(2,1)}, bf16[256,256]{1,0:T(8,128)(2,1)S(1)}, u32[]{:S(2)}) copy-start(bf16[256,256]{1,0:T(8,128)(2,1)S(1)} %reshape.245) | copy-start | bytes 393220
  80.2 9.1 %copy-start.28 = (bf16[256,256]{1,0:T(8,128)(2,1)}, bf16[256,256]{1,0:T(8,128)(2,1)S(1)}, u32[]{:S(2)}) copy-start(bf16[256,256]{1,0:T(8,128)(2,1)S(1)} %reshape.244) | copy-start | bytes 393220
  80.2 8.8 %copy-start.32 = (bf16[256,256]{1,0:T(8,128)(2,1)}, bf16[256,256]{1,0:T(8,128)(2,1)S(1)}, u32[]{:S(2)}) copy-start(bf16[256,256]{1,0:T(8,128)(2,1)S(1)} %reshape.243) | copy-start | bytes 393220
  80.3 8.5 %copy-start.36 = (bf16[256,256]{1,0:T(8,128)(2,1)}, bf16[256,256]{1,0:T(8,128)(2,1)S(1)}, u32[]{:S(2)}) copy-start(bf16[256,256]{1,0:T(8,128)(2,1)S(1)} %reshape.242) | copy-start | bytes 393220
  80.3 8.2 %copy-start.40 = (bf16[256,256]{1,0:T(8,128)(2,1)}, bf16[256,256]{1,0:T(8,128)(2,1)S(1)}, u32[]{:S(2)}) copy-start(bf16[256,256]{1,0:T(8,128)(2,1)S(1)} %reshape.241) | copy-start | bytes 393220
  81.3 7.0 %copy-start.44 = (bf16[256,256]{1,0:T(8,128)(2,1)}, bf16[256,256]{1,0:T(8,128)(2,1)S(1)}, u32[]{:S(2)}) copy-start(bf16[256,256]{1,0:T(8,128)(2,1)S(1)} %reshape.240) | copy-start | bytes 393220
  93.8 143.2 %all-reduce.4.cloned.1.call-start = ((), (), s32[]{:S(2)}) async-start(), calls=%async_computation.2 | async-start | bytes 3538944 | tf_op jit(solution)/shard_map/psum | solution.py:124
  108.7 23.1 %copy-start.1 = (bf16[27,256,256]{2,1,0:T(8,128)(2,1)S(1)}, bf16[27,256,256]{2,1,0:T(8,128)(2,1)}, u32[]{:S(2)}) copy-start(bf16[27,256,256]{2,1,0:T(8,128)(2,1)} %param.8) | copy-start | bytes 10616836
  131.8 6.9 %copy-start.43 = (bf16[256,256]{1,0:T(8,128)(2,1)S(1)}, bf16[256,256]{1,0:T(8,128)(2,1)}, u32[]{:S(2)}) copy-start(bf16[256,256]{1,0:T(8,128)(2,1)} %copy-done.42) | copy-start | bytes 393220
  131.8 7.1 %copy-start.39 = (bf16[256,256]{1,0:T(8,128)(2,1)S(1)}, bf16[256,256]{1,0:T(8,128)(2,1)}, u32[]{:S(2)}) copy-start(bf16[256,256]{1,0:T(8,128)(2,1)} %copy-done.38) | copy-start | bytes 393220
  131.8 7.3 %copy-start.35 = (bf16[256,256]{1,0:T(8,128)(2,1)S(1)}, bf16[256,256]{1,0:T(8,128)(2,1)}, u32[]{:S(2)}) copy-start(bf16[256,256]{1,0:T(8,128)(2,1)} %copy-done.34) | copy-start | bytes 393220
  131.8 7.6 %copy-start.31 = (bf16[256,256]{1,0:T(8,128)(2,1)S(1)}, bf16[256,256]{1,0:T(8,128)(2,1)}, u32[]{:S(2)}) copy-start(bf16[256,256]{1,0:T(8,128)(2,1)} %copy-done.30) | copy-start | bytes 393220
  133.0 6.6 %copy-start.21 = (bf16[256,256]{1,0:T(8,128)(2,1)S(1)}, bf16[256,256]{1,0:T(8,128)(2,1)}, u32[]{:S(2)}) copy-start(bf16[256,256]{1,0:T(8,128)(2,1)} %copy-done.20) | copy-start | bytes 393220
  134.1 5.7 %copy-start.17 = (bf16[256,256]{1,0:T(8,128)(2,1)S(1)}, bf16[256,256]{1,0:T(8,128)(2,1)}, u32[]{:S(2)}) copy-start(bf16[256,256]{1,0:T(8,128)(2,1)} %copy-done.16) | copy-start | bytes 393220
  135.3 4.7 %copy-start.19 = (bf16[256,256]{1,0:T(8,128)(2,1)S(1)}, bf16[256,256]{1,0:T(8,128)(2,1)}, u32[]{:S(2)}) copy-start(bf16[256,256]{1,0:T(8,128)(2,1)} %copy-done.18) | copy-start | bytes 393220
  136.4 3.8 %copy-start.9 = (bf16[256,256]{1,0:T(8,128)(2,1)S(1)}, bf16[256,256]{1,0:T(8,128)(2,1)}, u32[]{:S(2)}) copy-start(bf16[256,256]{1,0:T(8,128)(2,1)} %copy-done.8) | copy-start | bytes 393220
  137.6 2.9 %copy-start.5 = (bf16[256,256]{1,0:T(8,128)(2,1)S(1)}, bf16[256,256]{1,0:T(8,128)(2,1)}, u32[]{:S(2)}) copy-start(bf16[256,256]{1,0:T(8,128)(2,1)} %copy-done.4) | copy-start | bytes 393220
  141.3 2.6 %copy-start.70 = (bf16[256,256]{1,0:T(8,128)(2,1)S(1)}, bf16[256,256]{1,0:T(8,128)(2,1)}, u32[]{:S(2)}) copy-start(bf16[256,256]{1,0:T(8,128)(2,1)} %reshape.254) | copy-start | bytes 393220
  141.5 2.7 %copy-start.69 = (bf16[256,256]{1,0:T(8,128)(2,1)S(1)}, bf16[256,256]{1,0:T(8,128)(2,1)}, u32[]{:S(2)}) copy-start(bf16[256,256]{1,0:T(8,128)(2,1)} %reshape.255) | copy-start | bytes 393220
  141.7 2.7 %copy-start.68 = (bf16[256,256]{1,0:T(8,128)(2,1)S(1)}, bf16[256,256]{1,0:T(8,128)(2,1)}, u32[]{:S(2)}) copy-start(bf16[256,256]{1,0:T(8,128)(2,1)} %reshape.256) | copy-start | bytes 393220
  142.0 2.7 %copy-start.67 = (bf16[256,256]{1,0:T(8,128)(2,1)S(1)}, bf16[256,256]{1,0:T(8,128)(2,1)}, u32[]{:S(2)}) copy-start(bf16[256,256]{1,0:T(8,128)(2,1)} %reshape.257) | copy-start | bytes 393220
  142.2 2.8 %copy-start.66 = (bf16[256,256]{1,0:T(8,128)(2,1)S(1)}, bf16[256,256]{1,0:T(8,128)(2,1)}, u32[]{:S(2)}) copy-start(bf16[256,256]{1,0:T(8,128)(2,1)} %reshape.258) | copy-start | bytes 393220
  142.4 2.8 %copy-start.65 = (bf16[256,256]{1,0:T(8,128)(2,1)S(1)}, bf16[256,256]{1,0:T(8,128)(2,1)}, u32[]{:S(2)}) copy-start(bf16[256,256]{1,0:T(8,128)(2,1)} %reshape.259) | copy-start | bytes 393220
  142.6 2.8 %copy-start.64 = (bf16[256,256]{1,0:T(8,128)(2,1)S(1)}, bf16[256,256]{1,0:T(8,128)(2,1)}, u32[]{:S(2)}) copy-start(bf16[256,256]{1,0:T(8,128)(2,1)} %reshape.260) | copy-start | bytes 393220
  142.8 2.9 %copy-start.63 = (bf16[256,256]{1,0:T(8,128)(2,1)S(1)}, bf16[256,256]{1,0:T(8,128)(2,1)}, u32[]{:S(2)}) copy-start(bf16[256,256]{1,0:T(8,128)(2,1)} %reshape.261) | copy-start | bytes 393220
  143.0 2.9 %copy-start.60 = (bf16[256,256]{1,0:T(8,128)(2,1)S(1)}, bf16[256,256]{1,0:T(8,128)(2,1)}, u32[]{:S(2)}) copy-start(bf16[256,256]{1,0:T(8,128)(2,1)} %reshape.262) | copy-start | bytes 393220
  144.0 2.2 copy-start.58
  144.2 2.2 copy-start.59
  144.4 2.2 copy-start.54
  144.7 2.2 copy-start.53
  144.9 2.2 copy-start.52
  145.2 2.2 copy-start.57
  145.4 2.2 copy-start.56
  145.7 2.2 copy-start.55
  172.0 5.8 %copy-start.71 = (bf16[256,256]{1,0:T(8,128)(2,1)S(1)}, bf16[256,256]{1,0:T(8,128)(2,1)}, u32[]{:S(2)}) copy-start(bf16[256,256]{1,0:T(8,128)(2,1)} %reshape.277) | copy-start | bytes 393220
  172.0 6.1 %copy-start.51 = (bf16[256,256]{1,0:T(8,128)(2,1)S(1)}, bf16[256,256]{1,0:T(8,128)(2,1)}, u32[]{:S(2)}) copy-start(bf16[256,256]{1,0:T(8,128)(2,1)} %reshape.278) | copy-start | bytes 393220
  (18 other events, 32.3 us)
Sparse Core Ops, SparseCore 0:
  93.9 65.0 reduce-scatter.1
  161.5 75.4 all-reduce.3
where the time goes:
time: 248 us; the launch traced here: 247 us
  local copies, waits for them, and re-layouts  81.1 us (33%)
  waiting for transfers between devices  77.2 us (31%)
  matrix products  33.8 us (14%)
  starting transfers between devices  23.5 us (9%)
  between operations  16.1 us (6%)
  other arithmetic  15 us (6%)
    psum x1, waiting for transfers between devices, body(): grad_kernel = lax.psum(row_part, 'gy')  58.1 us
    reshape x52, local copies, waits for them, and re-layouts, window(): return padded[:, lower[0]:lower[0] + 4, lower[1]:lower[1] + 4, lower[2]:l...  40.1 us
    ppermute x4, starting transfers between devices, extended_2(): before = lax.ppermute(last, axis, up)  18 us
    gather x2, local copies, waits for them, and re-layouts, assemble_block(): jnp.take(bricks, brick_table.reshape(-1), axis=0)  14.4 us
    dot_general x27, matrix products, pull_conv(): lax.dot_general(window(cot_padded, shift, -1), kernel_weight[offset_index...  13 us
    dot_general x27, matrix products, forward_conv(): jnp.dot(window(padded, shift, 1), kernel_weight[offset_index], preferred_...  12.2 us
    reduce_scatter x1, waiting for transfers between devices, body(): lax.psum_scatter(kernel_part, 'gx', scatter_dimension=0, tiled=True)  9.7 us
    dot_general x27, matrix products, kernel_term(): lax.dot_general(window(padded, shift, 1), cot_flat, (((0,), (0,)), ((), (...  8.65 us
  transfers between devices with their start and end apart: 10, of which 5 were waited for; matrix products, arithmetic and copies ran while one was open for 31% of the time, Pallas kernels for 0%

commit v1 on v0

--- a/solution.py
+++ b/solution.py
@@ -121,7 +121,7 @@
     cot_flat = out_cotangent.reshape(slot_count * voxels, channels)
     kernel_part = kernel_term(padded, cot_flat)
     row_part = lax.psum_scatter(kernel_part, "gx", scatter_dimension=0, tiled=True)
-    grad_kernel = lax.psum(row_part, "gy")
+    grad_kernel = jnp.sum(lax.all_gather(row_part, "gy"), axis=0)
     cot_around = extended_2(out_cotangent, (("gx", 0), ("gy", 1)), 1)
     cot_padded = assemble_block(widen(cot_around, slot_count, voxels, channels), brick_table)
     grad_flat = pull_conv(cot_padded, kernel_weight).astype(jnp.bfloat16)

time: 248 us -> 300 us (1.21)
  waiting for transfers between devices: 77.2 us -> 130 us
  other arithmetic: 15 us -> 21.7 us
  local copies, waits for them, and re-layouts: 81.1 us -> 77.1 us
  matrix products: 33.8 us -> 30.3 us
    all_gather x0 -> x1, waiting for transfers between devices: none -> 114 us  [body(): grad_kernel = jnp.sum(lax.all_gather(row_part, 'gy'), axis=0)]
    psum x1 -> x0, waiting for transfers between devices: 58.1 us -> none  [body(): grad_kernel = lax.psum(row_part, 'gy')]
    dot_general x27, matrix products: 13 us -> 7.59 us  [pull_conv(): lax.dot_general(window(cot_padded, shift, -1), kernel_weight[offset_index...]
    reduce_sum x0 -> x1, other arithmetic: none -> 4.91 us  [body(): grad_kernel = jnp.sum(lax.all_gather(row_part, 'gy'), axis=0)]
    unnamed x149 -> x146, local copies, waits for them, and re-layouts: 5.58 us -> 2.15 us
  transfers between devices with their start and end apart: 10 -> 10, of which waited for: 5 -> 5; matrix products, arithmetic and copies ran while one was open for 31% -> 25% of each run, Pallas kernels for 0% -> 0%
where the time goes in v1:
time: 300 us; the launch traced here: 299 us
  waiting for transfers between devices  130 us (43%)
  local copies, waits for them, and re-layouts  77.1 us (26%)
  matrix products  30.3 us (10%)
  starting transfers between devices  23.5 us (8%)
  other arithmetic  21.7 us (7%)
  between operations  16.1 us (5%)
    all_gather x1, waiting for transfers between devices, body(): grad_kernel = jnp.sum(lax.all_gather(row_part, 'gy'), axis=0)  114 us
    reshape x52, local copies, waits for them, and re-layouts, window(): return padded[:, lower[0]:lower[0] + 4, lower[1]:lower[1] + 4, lower[2]:l...  39.5 us
    ppermute x4, starting transfers between devices, extended_2(): before = lax.ppermute(last, axis, up)  18 us
    dot_general x27, matrix products, forward_conv(): jnp.dot(window(padded, shift, 1), kernel_weight[offset_index], preferred_...  14.9 us
    gather x2, local copies, waits for them, and re-layouts, assemble_block(): jnp.take(bricks, brick_table.reshape(-1), axis=0)  14.2 us
    select_n x2, other arithmetic, assemble_block(): jnp.take(bricks, brick_table.reshape(-1), axis=0)  8.19 us
    slice x6, local copies, waits for them, and re-layouts, window(): padded[:, lower[0]:lower[0] + 4, lower[1]:lower[1] + 4, lower[2]:lower[2]...  7.99 us
    dot_general x27, matrix products, kernel_term(): lax.dot_general(window(padded, shift, 1), cot_flat, (((0,), (0,)), ((), (...  7.75 us
  transfers between devices with their start and end apart: 10, of which 5 were waited for; matrix products, arithmetic and copies ran while one was open for 25% of the time, Pallas kernels for 0%

profile of v1, /device:TPU:0, one launch (start us, length us, event | category | flops | bytes accessed | tf_op | source)
XLA Modules:
  0.0 298.7 jit_solution(11273732983484029783)
XLA Ops:
  7.2 2.4 collective-permute-start
  9.6 1.3 collective-permute-start.1
  10.9 1.3 collective-permute-start.5
  12.2 5.8 %collective-permute-start.4 = (bf16[1,1,4,64,256]{4,3,2,1,0:T(8,128)(2,1)}, bf16[1,1,4,64,256]{4,3,2,1,0:T(8,128)(2,1)S(1)}, u32[]{:S(2)}, u32[]{:S(2)}) collective-permute-start(bf16[1,1,4,64,256]{4,3,2,1,0:T(8,128)(2,1)} %param.9), channel_id=1, source_target_pairs={{0,4},{4,8},{8,12},{1,5},{5,9},{9,13},{2,6},{6,10},{10,14},{3,7},{... | collective-permute-start | bytes 393224 | tf_op jit(solution)/shard_map/ppermute | solution.py:23
  18.8 0.9 constant_dynamic-update-slice_fusion.1
  19.7 1.3 collective-permute-start.3
  21.0 4.6 %collective-permute-start.2 = (bf16[3,1,4,64,256]{4,3,2,1,0:T(8,128)(2,1)S(1)}, bf16[3,1,4,64,256]{4,3,2,1,0:T(8,128)(2,1)S(1)}, u32[]{:S(2)}, u32[]{:S(2)}) collective-permute-start(bf16[3,1,4,64,256]{4,3,2,1,0:T(8,128)(2,1)S(1)} %constant_dynamic-update-slice_fusion), channel_id=1, source_target_pairs={{0,1},{1,2},{2,3},{4,5},{5,6},{6,7},{8,9},{9,10},{10,11},{12,13},{... | collective-permute-start | bytes 1179656 | tf_op jit(solution)/shard_map/ppermute | solution.py:23
  25.6 0.9 constant_dynamic-update-slice_fusion.4
  26.6 1.3 collective-permute-start.7
  27.9 5.3 %collective-permute-start.6 = (bf16[3,1,4,64,256]{4,3,2,1,0:T(8,128)(2,1)S(1)}, bf16[3,1,4,64,256]{4,3,2,1,0:T(8,128)(2,1)}, u32[]{:S(2)}, u32[]{:S(2)}) collective-permute-start(bf16[3,1,4,64,256]{4,3,2,1,0:T(8,128)(2,1)S(1)} %constant_dynamic-update-slice_fusion.3), channel_id=1, source_target_pairs={{0,1},{1,2},{2,3},{4,5},{5,6},{6,7},{8,9},{9,10},{10,11},{12,13},{... | collective-permute-start | bytes 1179656 | tf_op jit(solution)/shard_map/ppermute | solution.py:23
  33.2 1.5 collective-permute-done.2
  35.2 6.1 %collective-permute-done.7 = bf16[3,1,4,64,256]{4,3,2,1,0:T(8,128)(2,1)S(1)} collective-permute-done((bf16[3,1,4,64,256]{4,3,2,1,0:T(8,128)(2,1)S(1)}, bf16[3,1,4,64,256]{4,3,2,1,0:T(8,128)(2,1)S(1)}, u32[]{:S(2)}, u32[]{:S(2)}) %collective-permute-start.7) | collective-permute-done | bytes 393248 | tf_op jit(solution)/shard_map/ppermute | solution.py:24
  41.3 1.8 collective-permute-done.6
  43.1 1.1 pad_maximum_fusion.1
  44.2 1.2 concatenate.194
  45.4 2.5 reshape.251
  47.9 7.1 %gather_fusion.1 = bf16[108,4,4,4,256]{4,3,2,1,0:T(4,128)(2,1)} fusion(bf16[37,4,4,4,256]{4,3,2,1,0:T(4,128)(2,1)S(1)} %reshape.251, s32[1024]{0:T(1024)S(1)} %pad_clamp_fusion), kind=kCustom, calls=%fused_computation.1.clone | custom fusion | bytes 7078320 | tf_op jit(solution)/shard_map/jit(_take)/gather | solution.py:33
  55.0 7.1 %gather_fusion = bf16[108,4,4,4,256]{4,3,2,1,0:T(4,128)(2,1)} fusion(bf16[37,4,4,4,256]{4,3,2,1,0:T(4,128)(2,1)S(1)} %reshape.221, s32[1024]{0:T(1024)S(1)} %pad_clamp_fusion), kind=kCustom, calls=%fused_computation.clone | custom fusion | bytes 7078320 | tf_op jit(solution)/shard_map/jit(_take)/gather | solution.py:33
  62.2 8.2 %broadcast_select_fusion = (bf16[108,4,4,4,256]{4,3,2,1,0:T(4,128)(2,1)}, bf16[108,4,4,4,256]{4,3,2,1,0:T(4,128)(2,1)S(1)}) fusion(bf16[108,4,4,4,256]{4,3,2,1,0:T(4,128)(2,1)} %gather_fusion.1, pred[108]{0:T(512)(128)(4,1)S(1)} %compare_and_fusion, bf16[108,4,4,4,256]{4,3,2,1,0:T(4,128)(2,1)} %gather_fusion), kind=kLoop, calls=%fused_computation.3 | loop fusion | flops 3538944 | bytes 14155884 | tf_op jit(solution)/shard_map/jit(_take)/select_n | solution.py:33
  75.7 1.3 fusion.116
  77.0 0.9 reshape.248
  78.0 1.0 reshape.247
  79.3 1.0 reshape.240
  80.3 1.2 convolution_dynamic-update-slice_fusion.26
  81.5 1.1 convolution_dynamic-update-slice_fusion.25
  88.5 3.4 %broadcast_multiply_fusion = f32[6912,256]{1,0:T(8,128)} fusion(f32[6912,256]{1,0:T(8,128)S(1)} %convolution_dynamic-update-slice_fusion), kind=kLoop, calls=%fused_computation.2 | loop fusion | flops 1769472 | bytes 14155776 | tf_op jit(solution)/shard_map/mul | solution.py:105
  92.1 1.0 fusion.112
  93.8 1.1 slice_bitcast_fusion.1
  103.3 0.9 slice_bitcast_fusion.39
  107.0 1.3 maximum_maximum_fusion.1
  108.3 1.4 fusion.114
  109.8 1.8 reshape.278
  111.5 1.6 reshape.277
  113.1 1.6 reshape.276
  114.7 1.7 reshape.275
  116.4 1.6 reshape.274
  118.0 1.6 reshape.273
  119.6 1.6 reshape.272
  121.2 1.6 reshape.271
  122.8 1.6 reshape.270
  124.4 3.9 %fusion.115 = (bf16[4,4,4,4,256]{4,3,2,1,0:T(4,128)(2,1)}, bf16[4,4,4,4,256]{4,3,2,1,0:T(4,128)(2,1)}, bf16[4,4,4,4,256]{4,3,2,1,0:T(4,128)(2,1)}, bf16[4,4,4,4,...) fusion(bf16[4,5,6,6,256]{4,3,2,1,0:T(8,128)(2,1)} %get-tuple-el, ...), kind=kLoop, calls=%fused_computation.284 | loop fusion | bytes 2359296 | tf_op jit(solution)/shard_map/slice | solution.py:64
  128.2 1.6 reshape.261
  129.8 1.6 reshape.260
  131.4 1.6 reshape.259
  133.0 1.6 reshape.258
  134.6 1.6 reshape.257
  136.2 1.6 reshape.256
  137.8 1.6 reshape.255
  139.4 1.6 reshape.254
  141.0 1.6 reshape.253
  142.6 1.1 fusion.56
  143.8 1.1 convolution_add_fusion.51
  144.9 1.1 convolution_add_fusion.50
  146.0 1.1 convolution_add_fusion.49
  147.1 1.1 convolution_add_fusion.48
  149.0 0.9 convolution_add_fusion.43
  149.9 7.1 %reduce-scatter.2.cloned.1.call-done = f32[1728,256]{1,0:T(8,128)} async-done(((f32[6912,256]{1,0:T(8,128)}), f32[1728,256]{1,0:T(8,128)}) %reduce-scatter.2.cloned.1.call-update) | async-done | bytes 1769488 | tf_op jit(solution)/shard_map/reduce_scatter | solution.py:123
  157.1 1.2 fusion.54
  158.3 1.2 convolution_add_fusion.42
  159.6 1.1 convolution_add_fusion.41
  160.7 1.1 convolution_add_fusion.40
  161.9 1.1 convolution_add_fusion.39
  173.5 113.5 %all-gather.3.cloned.1.call-done = f32[6912,256]{1,0:T(8,128)} async-done(((f32[1728,256]{1,0:T(8,128)}), f32[6912,256]{1,0:T(8,128)}) %all-gather.3.cloned.1.call-update) | async-done | bytes 7077904 | tf_op jit(solution)/shard_map/all_gather | solution.py:124
  287.0 4.9 %reduce_sum.9 = f32[1728,256]{1,0:T(8,128)} reduce(f32[4,1728,256]{2,1,0:T(8,128)} %bitcast.424, f32[]{:T(128)} %constant.2.clone.1), dimensions={0}, to_apply=%region_1.3 | reduce | flops 1327104 | bytes 8847364 | tf_op jit(solution)/shard_map/reduce_sum | solution.py:124
  (292 shorter events, 34.8 us)
Async XLA Ops:
  7.2 149.9 %reduce-scatter.2.cloned.1.call-start = ((), (), s32[]{:S(2)}) async-start(), calls=%async_computation.1 | async-start | bytes 8847360 | tf_op jit(solution)/shard_map/reduce_scatter | solution.py:123
  7.2 11.6 %collective-permute-start = (bf16[1,1,4,64,256]{4,3,2,1,0:T(8,128)(2,1)}, bf16[1,1,4,64,256]{4,3,2,1,0:T(8,128)(2,1)S(1)}, u32[]{:S(2)}, u32[]{:S(2)}) collective-permute-start(bf16[1,1,4,64,256]{4,3,2,1,0:T(8,128)(2,1)} %param.6), channel_id=1, source_target_pairs={{0,4},{4,8},{8,12},{1,5},{5,9},{9,13},{2,6},{6,10},{10,14},{3,7},{... | collective-permute-start | bytes 393224 | tf_op jit(solution)/shard_map/ppermute | solution.py:23
  9.6 10.1 %collective-permute-start.1 = (bf16[1,1,4,64,256]{4,3,2,1,0:T(8,128)(2,1)}, bf16[1,1,4,64,256]{4,3,2,1,0:T(8,128)(2,1)S(1)}, u32[]{:S(2)}, u32[]{:S(2)}) collective-permute-start(bf16[1,1,4,64,256]{4,3,2,1,0:T(8,128)(2,1)} %param.6), channel_id=1, source_target_pairs={{4,0},{8,4},{12,8},{5,1},{9,5},{13,9},{6,2},{10,6},{14,10},{7,3},{... | collective-permute-start | bytes 393224 | tf_op jit(solution)/shard_map/ppermute | solution.py:24
  10.9 15.7 %collective-permute-start.5 = (bf16[1,1,4,64,256]{4,3,2,1,0:T(8,128)(2,1)}, bf16[1,1,4,64,256]{4,3,2,1,0:T(8,128)(2,1)S(1)}, u32[]{:S(2)}, u32[]{:S(2)}) collective-permute-start(bf16[1,1,4,64,256]{4,3,2,1,0:T(8,128)(2,1)} %param.9), channel_id=1, source_target_pairs={{4,0},{8,4},{12,8},{5,1},{9,5},{13,9},{6,2},{10,6},{14,10},{7,3},{... | collective-permute-start | bytes 393224 | tf_op jit(solution)/shard_map/ppermute | solution.py:24
  12.2 13.4 %collective-permute-start.4 = (bf16[1,1,4,64,256]{4,3,2,1,0:T(8,128)(2,1)}, bf16[1,1,4,64,256]{4,3,2,1,0:T(8,128)(2,1)S(1)}, u32[]{:S(2)}, u32[]{:S(2)}) collective-permute-start(bf16[1,1,4,64,256]{4,3,2,1,0:T(8,128)(2,1)} %param.9), channel_id=1, source_target_pairs={{0,4},{4,8},{8,12},{1,5},{5,9},{9,13},{2,6},{6,10},{10,14},{3,7},{... | collective-permute-start | bytes 393224 | tf_op jit(solution)/shard_map/ppermute | solution.py:23
  19.7 13.5 %collective-permute-start.3 = (bf16[3,1,4,64,256]{4,3,2,1,0:T(8,128)(2,1)S(1)}, bf16[3,1,4,64,256]{4,3,2,1,0:T(8,128)(2,1)S(1)}, u32[]{:S(2)}, u32[]{:S(2)}) collective-permute-start(bf16[3,1,4,64,256]{4,3,2,1,0:T(8,128)(2,1)S(1)} %constant_dynamic-update-slice_fusion), channel_id=1, source_target_pairs={{1,0},{2,1},{3,2},{5,4},{6,5},{7,6},{9,8},{10,9},{11,10},{13,12},{... | collective-permute-start | bytes 1179656 | tf_op jit(solution)/shard_map/ppermute | solution.py:24
  21.0 13.6 %collective-permute-start.2 = (bf16[3,1,4,64,256]{4,3,2,1,0:T(8,128)(2,1)S(1)}, bf16[3,1,4,64,256]{4,3,2,1,0:T(8,128)(2,1)S(1)}, u32[]{:S(2)}, u32[]{:S(2)}) collective-permute-start(bf16[3,1,4,64,256]{4,3,2,1,0:T(8,128)(2,1)S(1)} %constant_dynamic-update-slice_fusion), channel_id=1, source_target_pairs={{0,1},{1,2},{2,3},{4,5},{5,6},{6,7},{8,9},{9,10},{10,11},{12,13},{... | collective-permute-start | bytes 1179656 | tf_op jit(solution)/shard_map/ppermute | solution.py:23
  26.6 14.7 %collective-permute-start.7 = (bf16[3,1,4,64,256]{4,3,2,1,0:T(8,128)(2,1)S(1)}, bf16[3,1,4,64,256]{4,3,2,1,0:T(8,128)(2,1)S(1)}, u32[]{:S(2)}, u32[]{:S(2)}) collective-permute-start(bf16[3,1,4,64,256]{4,3,2,1,0:T(8,128)(2,1)S(1)} %constant_dynamic-update-slice_fusion.3), channel_id=1, source_target_pairs={{1,0},{2,1},{3,2},{5,4},{6,5},{7,6},{9,8},{10,9},{11,10},{13,12},{... | collective-permute-start | bytes 1179656 | tf_op jit(solution)/shard_map/ppermute | solution.py:24
  27.9 15.2 %collective-permute-start.6 = (bf16[3,1,4,64,256]{4,3,2,1,0:T(8,128)(2,1)S(1)}, bf16[3,1,4,64,256]{4,3,2,1,0:T(8,128)(2,1)}, u32[]{:S(2)}, u32[]{:S(2)}) collective-permute-start(bf16[3,1,4,64,256]{4,3,2,1,0:T(8,128)(2,1)S(1)} %constant_dynamic-update-slice_fusion.3), channel_id=1, source_target_pairs={{0,1},{1,2},{2,3},{4,5},{5,6},{6,7},{8,9},{9,10},{10,11},{12,13},{... | collective-permute-start | bytes 1179656 | tf_op jit(solution)/shard_map/ppermute | solution.py:23
  70.9 14.3 %copy-start.4 = (bf16[256,256]{1,0:T(8,128)(2,1)}, bf16[256,256]{1,0:T(8,128)(2,1)S(1)}, u32[]{:S(2)}) copy-start(bf16[256,256]{1,0:T(8,128)(2,1)S(1)} %reshape_squeeze.12) | copy-start | bytes 393220
  71.2 14.2 %copy-start.5 = (bf16[256,256]{1,0:T(8,128)(2,1)}, bf16[256,256]{1,0:T(8,128)(2,1)S(1)}, u32[]{:S(2)}) copy-start(bf16[256,256]{1,0:T(8,128)(2,1)S(1)} %reshape.236) | copy-start | bytes 393220
  71.3 13.7 %copy-start.7 = (bf16[256,256]{1,0:T(8,128)(2,1)}, bf16[256,256]{1,0:T(8,128)(2,1)S(1)}, u32[]{:S(2)}) copy-start(bf16[256,256]{1,0:T(8,128)(2,1)S(1)} %reshape.235) | copy-start | bytes 393220
  72.7 13.5 %copy-start.8 = (bf16[256,256]{1,0:T(8,128)(2,1)}, bf16[256,256]{1,0:T(8,128)(2,1)S(1)}, u32[]{:S(2)}) copy-start(bf16[256,256]{1,0:T(8,128)(2,1)S(1)} %reshape.239) | copy-start | bytes 393220
  72.7 13.2 %copy-start.10 = (bf16[256,256]{1,0:T(8,128)(2,1)}, bf16[256,256]{1,0:T(8,128)(2,1)S(1)}, u32[]{:S(2)}) copy-start(bf16[256,256]{1,0:T(8,128)(2,1)S(1)} %reshape.238) | copy-start | bytes 393220
  72.8 12.9 %copy-start.12 = (bf16[256,256]{1,0:T(8,128)(2,1)}, bf16[256,256]{1,0:T(8,128)(2,1)S(1)}, u32[]{:S(2)}) copy-start(bf16[256,256]{1,0:T(8,128)(2,1)S(1)} %reshape.237) | copy-start | bytes 393220
  72.8 11.4 %copy-start.16 = (bf16[256,256]{1,0:T(8,128)(2,1)}, bf16[256,256]{1,0:T(8,128)(2,1)S(1)}, u32[]{:S(2)}) copy-start(bf16[256,256]{1,0:T(8,128)(2,1)S(1)} %reshape.232) | copy-start | bytes 393220
  72.9 11.6 %copy-start.14 = (bf16[256,256]{1,0:T(8,128)(2,1)}, bf16[256,256]{1,0:T(8,128)(2,1)S(1)}, u32[]{:S(2)}) copy-start(bf16[256,256]{1,0:T(8,128)(2,1)S(1)} %reshape.233) | copy-start | bytes 393220
  72.9 11.8 %copy-start.15 = (bf16[256,256]{1,0:T(8,128)(2,1)}, bf16[256,256]{1,0:T(8,128)(2,1)S(1)}, u32[]{:S(2)}) copy-start(bf16[256,256]{1,0:T(8,128)(2,1)S(1)} %reshape.234) | copy-start | bytes 393220
  73.9 6.3 %copy-start = (bf16[1,1,4,64,256]{4,3,2,1,0:T(8,128)(2,1)S(1)}, bf16[1,1,4,64,256]{4,3,2,1,0:T(8,128)(2,1)}, u32[]{:S(2)}) copy-start(bf16[1,1,4,64,256]{4,3,2,1,0:T(8,128)(2,1)} %param.9) | copy-start | bytes 393220
  74.0 10.0 %copy-start.32 = (bf16[256,256]{1,0:T(8,128)(2,1)}, bf16[256,256]{1,0:T(8,128)(2,1)S(1)}, u32[]{:S(2)}) copy-start(bf16[256,256]{1,0:T(8,128)(2,1)S(1)} %reshape.231) | copy-start | bytes 393220
  74.0 9.7 %copy-start.36 = (bf16[256,256]{1,0:T(8,128)(2,1)}, bf16[256,256]{1,0:T(8,128)(2,1)S(1)}, u32[]{:S(2)}) copy-start(bf16[256,256]{1,0:T(8,128)(2,1)S(1)} %reshape.230) | copy-start | bytes 393220
  74.1 9.5 %copy-start.38 = (bf16[256,256]{1,0:T(8,128)(2,1)}, bf16[256,256]{1,0:T(8,128)(2,1)S(1)}, u32[]{:S(2)}) copy-start(bf16[256,256]{1,0:T(8,128)(2,1)S(1)} %reshape.229) | copy-start | bytes 393220
  74.1 9.2 %copy-start.40 = (bf16[256,256]{1,0:T(8,128)(2,1)}, bf16[256,256]{1,0:T(8,128)(2,1)S(1)}, u32[]{:S(2)}) copy-start(bf16[256,256]{1,0:T(8,128)(2,1)S(1)} %reshape.228) | copy-start | bytes 393220
  74.2 8.9 %copy-start.42 = (bf16[256,256]{1,0:T(8,128)(2,1)}, bf16[256,256]{1,0:T(8,128)(2,1)S(1)}, u32[]{:S(2)}) copy-start(bf16[256,256]{1,0:T(8,128)(2,1)S(1)} %reshape.227) | copy-start | bytes 393220
  74.2 8.6 %copy-start.43 = (bf16[256,256]{1,0:T(8,128)(2,1)}, bf16[256,256]{1,0:T(8,128)(2,1)S(1)}, u32[]{:S(2)}) copy-start(bf16[256,256]{1,0:T(8,128)(2,1)S(1)} %reshape.226) | copy-start | bytes 393220
  74.3 8.8 %copy-start.44 = (bf16[256,256]{1,0:T(8,128)(2,1)}, bf16[256,256]{1,0:T(8,128)(2,1)S(1)}, u32[]{:S(2)}) copy-start(bf16[256,256]{1,0:T(8,128)(2,1)S(1)} %reshape.225) | copy-start | bytes 393220
  78.0 10.3 %copy-start.2 = (bf16[256,256]{1,0:T(8,128)(2,1)}, bf16[256,256]{1,0:T(8,128)(2,1)S(1)}, u32[]{:S(2)}) copy-start(bf16[256,256]{1,0:T(8,128)(2,1)S(1)} %reshape.248) | copy-start | bytes 393220
  79.0 9.1 %copy-start.18 = (bf16[256,256]{1,0:T(8,128)(2,1)}, bf16[256,256]{1,0:T(8,128)(2,1)S(1)}, u32[]{:S(2)}) copy-start(bf16[256,256]{1,0:T(8,128)(2,1)S(1)} %reshape.247) | copy-start | bytes 393220
  79.0 8.8 %copy-start.20 = (bf16[256,256]{1,0:T(8,128)(2,1)}, bf16[256,256]{1,0:T(8,128)(2,1)S(1)}, u32[]{:S(2)}) copy-start(bf16[256,256]{1,0:T(8,128)(2,1)S(1)} %reshape.246) | copy-start | bytes 393220
  79.1 8.5 %copy-start.22 = (bf16[256,256]{1,0:T(8,128)(2,1)}, bf16[256,256]{1,0:T(8,128)(2,1)S(1)}, u32[]{:S(2)}) copy-start(bf16[256,256]{1,0:T(8,128)(2,1)S(1)} %reshape.245) | copy-start | bytes 393220
  79.1 8.2 %copy-start.24 = (bf16[256,256]{1,0:T(8,128)(2,1)}, bf16[256,256]{1,0:T(8,128)(2,1)S(1)}, u32[]{:S(2)}) copy-start(bf16[256,256]{1,0:T(8,128)(2,1)S(1)} %reshape.244) | copy-start | bytes 393220
  79.2 7.9 %copy-start.26 = (bf16[256,256]{1,0:T(8,128)(2,1)}, bf16[256,256]{1,0:T(8,128)(2,1)S(1)}, u32[]{:S(2)}) copy-start(bf16[256,256]{1,0:T(8,128)(2,1)S(1)} %reshape.243) | copy-start | bytes 393220
  79.2 7.6 %copy-start.28 = (bf16[256,256]{1,0:T(8,128)(2,1)}, bf16[256,256]{1,0:T(8,128)(2,1)S(1)}, u32[]{:S(2)}) copy-start(bf16[256,256]{1,0:T(8,128)(2,1)S(1)} %reshape.242) | copy-start | bytes 393220
  79.3 7.3 %copy-start.30 = (bf16[256,256]{1,0:T(8,128)(2,1)}, bf16[256,256]{1,0:T(8,128)(2,1)S(1)}, u32[]{:S(2)}) copy-start(bf16[256,256]{1,0:T(8,128)(2,1)S(1)} %reshape.241) | copy-start | bytes 393220
  80.3 6.1 %copy-start.34 = (bf16[256,256]{1,0:T(8,128)(2,1)}, bf16[256,256]{1,0:T(8,128)(2,1)S(1)}, u32[]{:S(2)}) copy-start(bf16[256,256]{1,0:T(8,128)(2,1)S(1)} %reshape.240) | copy-start | bytes 393220
  91.9 195.1 %all-gather.3.cloned.1.call-start = ((), (), s32[]{:S(2)}) async-start(), calls=%async_computation.2 | async-start | bytes 8847360 | tf_op jit(solution)/shard_map/all_gather | solution.py:124
  109.8 32.8 %copy-start.1 = (bf16[27,256,256]{2,1,0:T(8,128)(2,1)S(1)}, bf16[27,256,256]{2,1,0:T(8,128)(2,1)}, u32[]{:S(2)}) copy-start(bf16[27,256,256]{2,1,0:T(8,128)(2,1)} %param.8) | copy-start | bytes 10616836
  142.6 5.6 %copy-start.41 = (bf16[256,256]{1,0:T(8,128)(2,1)S(1)}, bf16[256,256]{1,0:T(8,128)(2,1)}, u32[]{:S(2)}) copy-start(bf16[256,256]{1,0:T(8,128)(2,1)} %copy-done.40) | copy-start | bytes 393220
  142.6 5.8 %copy-start.39 = (bf16[256,256]{1,0:T(8,128)(2,1)S(1)}, bf16[256,256]{1,0:T(8,128)(2,1)}, u32[]{:S(2)}) copy-start(bf16[256,256]{1,0:T(8,128)(2,1)} %copy-done.38) | copy-start | bytes 393220
  142.6 6.0 %copy-start.37 = (bf16[256,256]{1,0:T(8,128)(2,1)S(1)}, bf16[256,256]{1,0:T(8,128)(2,1)}, u32[]{:S(2)}) copy-start(bf16[256,256]{1,0:T(8,128)(2,1)} %copy-done.36) | copy-start | bytes 393220
  142.6 6.2 %copy-start.33 = (bf16[256,256]{1,0:T(8,128)(2,1)S(1)}, bf16[256,256]{1,0:T(8,128)(2,1)}, u32[]{:S(2)}) copy-start(bf16[256,256]{1,0:T(8,128)(2,1)} %copy-done.32) | copy-start | bytes 393220
  142.6 6.4 %copy-start.17 = (bf16[256,256]{1,0:T(8,128)(2,1)S(1)}, bf16[256,256]{1,0:T(8,128)(2,1)}, u32[]{:S(2)}) copy-start(bf16[256,256]{1,0:T(8,128)(2,1)} %copy-done.16) | copy-start | bytes 393220
  157.1 5.9 %copy-start.6 = (bf16[256,256]{1,0:T(8,128)(2,1)S(1)}, bf16[256,256]{1,0:T(8,128)(2,1)}, u32[]{:S(2)}) copy-start(bf16[256,256]{1,0:T(8,128)(2,1)} %copy-done.5) | copy-start | bytes 393220
  157.1 6.1 %copy-start.13 = (bf16[256,256]{1,0:T(8,128)(2,1)S(1)}, bf16[256,256]{1,0:T(8,128)(2,1)}, u32[]{:S(2)}) copy-start(bf16[256,256]{1,0:T(8,128)(2,1)} %copy-done.12) | copy-start | bytes 393220
  157.1 6.3 %copy-start.11 = (bf16[256,256]{1,0:T(8,128)(2,1)S(1)}, bf16[256,256]{1,0:T(8,128)(2,1)}, u32[]{:S(2)}) copy-start(bf16[256,256]{1,0:T(8,128)(2,1)} %copy-done.10) | copy-start | bytes 393220
  157.1 6.6 %copy-start.9 = (bf16[256,256]{1,0:T(8,128)(2,1)S(1)}, bf16[256,256]{1,0:T(8,128)(2,1)}, u32[]{:S(2)}) copy-start(bf16[256,256]{1,0:T(8,128)(2,1)} %copy-done.8) | copy-start | bytes 393220
  157.1 6.8 %copy-start.35 = (bf16[256,256]{1,0:T(8,128)(2,1)S(1)}, bf16[256,256]{1,0:T(8,128)(2,1)}, u32[]{:S(2)}) copy-start(bf16[256,256]{1,0:T(8,128)(2,1)} %copy-done.34) | copy-start | bytes 393220
  158.3 5.8 %copy-start.31 = (bf16[256,256]{1,0:T(8,128)(2,1)S(1)}, bf16[256,256]{1,0:T(8,128)(2,1)}, u32[]{:S(2)}) copy-start(bf16[256,256]{1,0:T(8,128)(2,1)} %copy-done.30) | copy-start | bytes 393220
  159.6 4.7 %copy-start.29 = (bf16[256,256]{1,0:T(8,128)(2,1)S(1)}, bf16[256,256]{1,0:T(8,128)(2,1)}, u32[]{:S(2)}) copy-start(bf16[256,256]{1,0:T(8,128)(2,1)} %copy-done.28) | copy-start | bytes 393220
  160.7 3.8 %copy-start.27 = (bf16[256,256]{1,0:T(8,128)(2,1)S(1)}, bf16[256,256]{1,0:T(8,128)(2,1)}, u32[]{:S(2)}) copy-start(bf16[256,256]{1,0:T(8,128)(2,1)} %copy-done.26) | copy-start | bytes 393220
  161.9 2.9 copy-start.25
  163.9 2.6 copy-start.70
  164.1 2.6 copy-start.69
  164.3 2.6 copy-start.68
  164.5 2.7 copy-start.67
  164.7 2.7 copy-start.66
  165.0 2.7 copy-start.65
  165.2 2.8 copy-start.64
  165.4 2.8 copy-start.63
  165.6 2.8 copy-start.54
  166.7 2.2 copy-start.53
  167.2 2.2 copy-start.46
  167.7 2.2 copy-start.51
  168.2 2.2 copy-start.49
  (17 other events, 36.3 us)
Sparse Core Ops, SparseCore 0:
  92.0 65.0 reduce-scatter.1
  158.7 128.2 all-gather.2
